TPU v7x, 32 devices: a whole 2x2x4 slice. The times are simulated.
32 devices in a mesh: energy: 8 (over z, y), cell: 4 (over x, core).
Axes of the slice: x: 2, y: 2, z: 4, core: 2. Of those that a mesh axis runs over, the one named last changes fastest.
Arguments:
- retarded: bfloat16 [4, 2, 32, 256, 256], P('cell', None, 'energy'), may hold values from -0.25 to 0.25
- sigma_lesser: bfloat16 [4, 2, 32, 256, 256], P('cell', None, 'energy'), may hold values from -6 to 6
- sigma_greater: bfloat16 [4, 2, 32, 256, 256], P('cell', None, 'energy'), may hold values from -6 to 6
- coulomb: bfloat16 [4, 3, 256, 256], P('cell'), may hold values from -0.21875 to 0.21875
Outputs:
- screened: bfloat16 [4, 2, 32, 256, 256], P('cell', None, 'energy')
All inputs are finite; a program needn't handle non-finite values.
Results may differ from a plain program's by a relative error of at most 0.009.
Values may be sent and summed in bfloat16 or wider, within the bound.
A program may use at most 64 MiB of HBM per device.

v0:
```python
import functools
import math

import jax
import jax.numpy as jnp
from jax import lax
from jax.experimental import pallas as pl
from jax.experimental.pallas import tpu as pltpu
from jax.sharding import PartitionSpec as P

MESH = pl.DeviceIdType.MESH
ROWS = 16
LANES = 128
QUARTERS = 4
DELAY = 6
LATE = 4
LAG = 0
SHIFT = 4
LEAD = 3
F32 = jnp.float32
BF16 = jnp.bfloat16


def nn(a, b):
    return jnp.dot(a, b, preferred_element_type=F32)


def nt(a, b):
    return lax.dot_general(a, b, (((1,), (1,)), ((), ())), preferred_element_type=F32)


def fused_kernel(
    n, cells, green_in, sig_l_in, sig_g_in, coulomb_in, out,
    green, sig_l, sig_g, coulomb, in_sem, coulomb_sem, send, recv, part, send_p, pol, total,
    send_sem, recv_sem, forward_send_sem, forward_recv_sem, relay_send_sem, relay_recv_sem, part_send_sem, part_recv_sem,
    ret_send_sem, ret_recv_sem, halo_send_sem, halo_recv_sem,
):
    me = lax.axis_index("energy")
    cell = lax.axis_index("cell")
    local = green.shape[1]
    norb = green.shape[2]
    width = n // QUARTERS
    half = 2 * width
    quarter, place = me // width, lax.rem(me, width)
    home = jnp.where(me < half, 1, 2)
    strip = norb // width
    col_parts = norb // LANES
    chunks = strip // ROWS * col_parts
    has_low = cell > 0
    has_high = cell < cells - 1

    def loads(e):
        return [
            pltpu.make_async_copy(source.at[:, e], held.at[:, e], in_sem.at[i, e])
            for i, (source, held) in enumerate(((green_in, green), (sig_l_in, sig_l), (sig_g_in, sig_g)))
        ]

    for e in range(local):
        for load in loads(e):
            load.start()
    coulomb_load = pltpu.make_async_copy(coulomb_in, coulomb, coulomb_sem)
    coulomb_load.start()

    barrier = pltpu.get_barrier_semaphore()

    @pl.loop(1, n)
    def _(k):
        pl.semaphore_signal(barrier, inc=1, device_id={"energy": lax.rem(me + k, n)}, device_id_type=MESH)

    @pl.when(has_low)
    def _():
        pl.semaphore_signal(barrier, inc=1, device_id={"cell": cell - 1}, device_id_type=MESH)

    @pl.when(has_high)
    def _():
        pl.semaphore_signal(barrier, inc=1, device_id={"cell": cell + 1}, device_id_type=MESH)

    def put(value, comp, e):
        value = value.astype(BF16).reshape(width, strip, norb)
        for q in range(chunks):
            r, c = divmod(q, col_parts)
            send[q, :, comp, e] = value[:, r * ROWS:(r + 1) * ROWS, c * LANES:(c + 1) * LANES]

    @pl.loop(0, local)
    def _(e):
        for load in loads(e):
            load.wait()
        g_re, g_im = green[0, e], green[1, e]
        l_re, l_im = sig_l[0, e], sig_l[1, e]
        half_re = (nn(g_re, l_re) - nn(g_im, l_im)).astype(BF16)
        half_im = (nn(g_re, l_im) + nn(g_im, l_re)).astype(BF16)
        put(nt(half_re, g_re) + nt(half_im, g_im), 0, e)
        put(nt(half_im, g_re) - nt(half_re, g_im), 1, e)
        s_re, s_im = sig_g[0, e], sig_g[1, e]
        half_re = (nn(g_re, s_re) - nn(g_im, s_im)).astype(BF16)
        half_im = (nn(g_re, s_im) + nn(g_im, s_re)).astype(BF16)
        put(nt(g_re, half_re) + nt(g_im, half_im), 2, e)
        put(nt(g_re, half_im) - nt(g_im, half_re), 3, e)

    pl.semaphore_wait(barrier, n - 1 + has_low.astype(jnp.int32) + has_high.astype(jnp.int32))


    def strip_copy(q, slot, where):
        return pltpu.make_async_remote_copy(
            src_ref=send.at[q, where], dst_ref=recv.at[q, slot],
            send_sem=send_sem.at[q, where], recv_sem=recv_sem.at[q, slot],
            device_id={"energy": quarter * width + where}, device_id_type=MESH,
        )

    def each_target(act):
        for where in range(width):
            pl.when(where != place)(functools.partial(act, where))

    lead = jnp.where(quarter == home, min(LEAD, chunks), chunks)

    @pl.loop(0, lead)
    def _(q):
        each_target(lambda where: strip_copy(q, me, where).start())

    def more(q):
        @pl.when(q + lead < chunks)
        def _():
            each_target(lambda where: strip_copy(q + lead, me, where).start())

    @pl.loop(0, chunks)
    def _(q):
        recv[q, me] = send[q, place]

    blank = jnp.zeros((2, local, ROWS, LANES), BF16)

    @pl.when(quarter == 1)
    def _():
        @pl.loop(0, chunks)
        def _(q):
            recv[q, half, 0:2] = blank

    @pl.when(quarter == 2)
    def _():
        @pl.loop(0, chunks)
        def _(q):
            recv[q, half - 1, 0:2] = blank
            recv[q, n, 0:2] = blank

    @pl.when(jnp.logical_not(has_low))
    def _():
        pol[0] = jnp.zeros_like(pol[0])

    @pl.when(jnp.logical_not(has_high))
    def _():
        pol[2] = jnp.zeros_like(pol[2])

    def spot(q):
        rows = pl.ds(pl.multiple_of(q // col_parts * ROWS, ROWS), ROWS)
        return rows, pl.ds(pl.multiple_of(q % col_parts * LANES, LANES), LANES)

    def forward_copy(q, kind):
        block = (q, pl.ds(quarter * width, width), slice(2 * kind, 2 * kind + 2))
        return pltpu.make_async_remote_copy(
            src_ref=recv.at[block], dst_ref=recv.at[block],
            send_sem=forward_send_sem.at[q, kind], recv_sem=forward_recv_sem.at[q, kind],
            device_id={"energy": home * width + place}, device_id_type=MESH,
        )

    def relay_copy(q, origin):
        block = (q, slice(origin * width, (origin + 1) * width), slice(2, 4))
        return pltpu.make_async_remote_copy(
            src_ref=recv.at[block], dst_ref=recv.at[block],
            send_sem=relay_send_sem.at[q, origin], recv_sem=relay_recv_sem.at[q, origin],
            device_id={"energy": 2 * width + place}, device_id_type=MESH,
        )

    def part_copy(q):
        return pltpu.make_async_remote_copy(
            src_ref=send_p.at[q, 0:half], dst_ref=part.at[q],
            send_sem=part_send_sem.at[q], recv_sem=part_recv_sem.at[q],
            device_id={"energy": width + place}, device_id_type=MESH,
        )

    def return_copy(q, where, owner):
        return pltpu.make_async_remote_copy(
            src_ref=send_p.at[q, owner], dst_ref=pol.at[1, :, :, where, *spot(q)],
            send_sem=ret_send_sem.at[q, owner], recv_sem=ret_recv_sem.at[q, where],
            device_id={"energy": owner}, device_id_type=MESH,
        )

    def halo_copy(q, slot, other):
        return pltpu.make_async_remote_copy(
            src_ref=pol.at[1, :, :, :, *spot(q)], dst_ref=pol.at[slot, :, :, :, *spot(q)],
            send_sem=halo_send_sem.at[q, slot // 2], recv_sem=halo_recv_sem.at[q, slot // 2],
            device_id={"cell": other}, device_id_type=MESH,
        )

    factor = 1.0 / math.sqrt(n * local)

    def correlate(q, b, first_step, last_step):
        def step(a, acc):
            first = [
                (recv[q, a + b + i // local, 0, i % local].astype(F32), recv[q, a + b + i // local, 1, i % local].astype(F32))
                for i in range(2 * local - 1)
            ]
            acc = list(acc)
            for e in range(local):
                x_re, x_im = recv[q, a, 2, e].astype(F32), recv[q, a, 3, e].astype(F32)
                for w in range(local):
                    y_re, y_im = first[e + w]
                    acc[2 * w] = acc[2 * w] + (y_re * x_re - y_im * x_im)
                    acc[2 * w + 1] = acc[2 * w + 1] + (y_re * x_im + y_im * x_re)
            return tuple(acc)

        zero = jnp.zeros((ROWS, LANES), F32)
        acc = lax.fori_loop(first_step, last_step, step, (zero,) * (2 * local))
        return [value * factor for value in acc]

    def hand_out(q, owner):
        @pl.when(owner != me)
        def _():
            return_copy(q, place, owner).start()

        @pl.when(owner == me)
        def _():
            pol[1, :, :, place, *spot(q)] = send_p[q, owner]

    def gather(q):
        each_target(lambda where: strip_copy(q, quarter * width + where, where).wait_recv())

    def halo(q):
        for where in range(width):
            @pl.when(home * width + where != me)
            def _():
                return_copy(q, where, 0).wait_recv()

        @pl.when(has_low)
        def _():
            halo_copy(q, 2, cell - 1).start()

        @pl.when(has_high)
        def _():
            halo_copy(q, 0, cell + 1).start()

    @pl.when(quarter == 2)
    def _():
        @pl.loop(0, chunks)
        def _(q):
            gather(q)
            more(q)
            forward_copy(q, 1).wait_recv()
            forward_copy(q, 0).wait_recv()
            relay_copy(q, 1).wait_recv()
            relay_copy(q, 0).wait_recv()

            @pl.loop(0, n)
            def _(b):
                acc = correlate(q, b, jnp.maximum(half - 1 - b, 0), n - b)
                for w in range(local):
                    send_p[q, b, 0, w] = acc[2 * w].astype(BF16)
                    send_p[q, b, 1, w] = acc[2 * w + 1].astype(BF16)

                @pl.when(b == half)
                def _():
                    part_copy(q).start()

                @pl.when(b >= half)
                def _():
                    hand_out(q, b)

            @pl.when(q >= LATE)
            def _():
                halo(q - LATE)

        for q in range(max(chunks - LATE, 0), chunks):
            halo(q)

    delay = min(DELAY, chunks)
    lag = min(LAG, delay)

    @pl.when(quarter == 1)
    def _():
        @pl.loop(0, chunks + delay + LATE)
        def _(t):
            @pl.when(t < chunks)
            def _():
                gather(t)
                relay_copy(t, 1).start()
                more(t)

            @pl.when(jnp.logical_and(t >= lag, t < chunks + lag))
            def _():
                forward_copy(t - lag, 1).wait_recv()
                relay_copy(t - lag, 0).start()

            @pl.when(jnp.logical_and(t >= delay, t < chunks + delay))
            def _():
                q = t - delay
                forward_copy(q, 0).wait_recv()
                part_copy(q).wait_recv()

                @pl.loop(0, half)
                def _(b):
                    acc = correlate(q, b, 0, half - b)
                    for w in range(local):
                        send_p[q, b, 0, w] = (acc[2 * w] + part[q, b, 0, w].astype(F32)).astype(BF16)
                        send_p[q, b, 1, w] = (acc[2 * w + 1] + part[q, b, 1, w].astype(F32)).astype(BF16)
                    hand_out(q, b)

            @pl.when(t >= delay + LATE)
            def _():
                halo(t - delay - LATE)

    @pl.when(quarter != home)
    def _():
        shift = jnp.where(quarter == 0, min(SHIFT, chunks), 0)

        @pl.loop(0, chunks + shift)
        def _(q):
            @pl.when(q < chunks)
            def _():
                gather(q)
                forward_copy(q, 1).start()

            @pl.when(q >= shift)
            def _():
                forward_copy(q - shift, 0).start()

        @pl.loop(0, chunks)
        def _(q):
            halo(q)

    def polarized(slot, c, e):
        return pol[slot, c, e].reshape(norb, norb)

    coulomb_load.wait()

    @pl.loop(0, local)
    def _(e):
        for c in range(2):
            total[c, e] = nn(coulomb[1], polarized(1, c, e))

    @pl.loop(0, chunks)
    def _(q):
        @pl.when(has_low)
        def _():
            halo_copy(q, 0, cell - 1).wait_recv()
            halo_copy(q, 2, cell - 1).wait_send()

        @pl.when(has_high)
        def _():
            halo_copy(q, 2, cell + 1).wait_recv()
            halo_copy(q, 0, cell + 1).wait_send()

    @pl.loop(0, local)
    def _(e):
        for c in range(2):
            summed = total[c, e] + nn(coulomb[0], polarized(0, c, e)) + nn(coulomb[2], polarized(2, c, e))
            out[c, e] = summed.astype(BF16)

    @pl.loop(0, chunks)
    def _(q):
        each_target(lambda where: strip_copy(q, me, where).wait_send())

        @pl.when(quarter != home)
        def _():
            forward_copy(q, 1).wait_send()
            forward_copy(q, 0).wait_send()

        @pl.when(quarter == 1)
        def _():
            relay_copy(q, 0).wait_send()
            relay_copy(q, 1).wait_send()

        @pl.when(quarter == 2)
        def _():
            part_copy(q).wait_send()

        @pl.when(quarter == home)
        def _():
            @pl.loop(0, half)
            def _(b):
                owner = (home - 1) * half + b

                @pl.when(owner != me)
                def _():
                    return_copy(q, place, owner).wait_send()


def fused(n, cells, retarded, sigma_lesser, sigma_greater, coulomb):
    green = retarded[0]
    local, norb = green.shape[1], green.shape[2]
    width = n // QUARTERS
    half = 2 * width
    strip = norb // width
    chunks = strip // ROWS * (norb // LANES)
    vmem = pl.BlockSpec(memory_space=pltpu.VMEM)
    dma = pltpu.SemaphoreType.DMA
    result = pl.pallas_call(
        functools.partial(fused_kernel, n, cells),
        out_shape=jax.ShapeDtypeStruct(green.shape, BF16),
        in_specs=[pl.BlockSpec(memory_space=pltpu.HBM)] * 4,
        out_specs=vmem,
        scratch_shapes=[
            pltpu.VMEM(green.shape, BF16),
            pltpu.VMEM(green.shape, BF16),
            pltpu.VMEM(green.shape, BF16),
            pltpu.VMEM(coulomb.shape[1:], BF16),
            dma((3, local)), dma,
            pltpu.VMEM((chunks, width, 4, local, ROWS, LANES), BF16),
            pltpu.VMEM((chunks, n + 1, 4, local, ROWS, LANES), BF16),
            pltpu.VMEM((chunks, half, 2, local, ROWS, LANES), BF16),
            pltpu.VMEM((chunks, n, 2, local, ROWS, LANES), BF16),
            pltpu.VMEM((3, 2, local, width, strip, norb), BF16),
            pltpu.VMEM((2, local, norb, norb), F32),
            dma((chunks, width)), dma((chunks, n)), dma((chunks, 2)), dma((chunks, 2)),
            dma((chunks, 2)), dma((chunks, 2)), dma((chunks,)), dma((chunks,)),
            dma((chunks, n)), dma((chunks, width)),
            dma((chunks, 2)), dma((chunks, 2)),
        ],
        compiler_params=pltpu.CompilerParams(
            collective_id=0, has_side_effects=True, vmem_limit_bytes=56 * 1024 * 1024
        ),
    )(green, sigma_lesser[0], sigma_greater[0], coulomb[0])
    return result[None]


def thin(n, cells, retarded, sigma_lesser, sigma_greater, coulomb):
    green = retarded[0]
    local = green.shape[1]

    def halves(sigma):
        def product(x, y):
            return jnp.einsum("eik,ekj->eij", x, y, preferred_element_type=F32)

        re = product(green[0], sigma[0]) - product(green[1], sigma[1])
        im = product(green[0], sigma[1]) + product(green[1], sigma[0])
        return re.astype(BF16), im.astype(BF16)

    def adjoint(x, y):
        return jnp.einsum("eik,ejk->eij", x, y, preferred_element_type=F32)

    re, im = halves(sigma_lesser[0])
    lesser = jnp.stack([adjoint(re, green[0]) + adjoint(im, green[1]), adjoint(im, green[0]) - adjoint(re, green[1])])
    re, im = halves(sigma_greater[0])
    greater = jnp.stack([adjoint(green[0], re) + adjoint(green[1], im), adjoint(green[0], im) - adjoint(green[1], re)])
    first = lax.all_to_all(lesser.astype(BF16), "energy", split_axis=2, concat_axis=1, tiled=True).astype(F32)
    second = lax.all_to_all(greater.astype(BF16), "energy", split_axis=2, concat_axis=1, tiled=True).astype(F32)
    energies = n * local
    padded = jnp.concatenate([first, jnp.zeros_like(first)], axis=1)

    def lag(w):
        y = lax.dynamic_slice_in_dim(padded, w, energies, axis=1)
        re = jnp.sum(y[0] * second[0] - y[1] * second[1], axis=0)
        im = jnp.sum(y[0] * second[1] + y[1] * second[0], axis=0)
        return (jnp.stack([re, im]) / math.sqrt(energies)).astype(BF16)

    polarized = jnp.swapaxes(lax.map(lag, jnp.arange(energies)), 0, 1)
    polarized = lax.all_to_all(polarized, "energy", split_axis=1, concat_axis=2, tiled=True)
    up = [(i, i + 1) for i in range(cells - 1)]
    low = lax.ppermute(polarized, "cell", up)
    high = lax.ppermute(polarized, "cell", [(t, s) for s, t in up])
    stacked = jnp.stack([low, polarized, high])
    summed = jnp.einsum("dik,dcekj->ceij", coulomb[0], stacked, preferred_element_type=F32)
    return summed.astype(BF16)[None]


def solution(mesh):
    n, cells = mesh.shape["energy"], mesh.shape["cell"]

    def on_device(retarded, sigma_lesser, sigma_greater, coulomb):
        norb = retarded.shape[-1]
        whole_tiles = n % QUARTERS == 0 and norb % LANES == 0 and norb % (n // QUARTERS * ROWS) == 0
        plan = fused if whole_tiles else thin
        return plan(n, cells, retarded, sigma_lesser, sigma_greater, coulomb)

    in_specs = (
        P("cell", None, "energy", None, None),
        P("cell", None, "energy", None, None),
        P("cell", None, "energy", None, None),
        P("cell", None, None, None),
    )
    out_specs = P("cell", None, "energy", None, None)
    return jax.shard_map(
        on_device, mesh=mesh, in_specs=in_specs, out_specs=out_specs, check_vma=False
    )
```

profile of v0, /device:TPU:1, one launch (start us, length us, event | category | flops | bytes accessed | tf_op | source)
XLA Modules:
  0.0 80.6 jit_solution(3175387292632839149)
XLA Ops:
  0.0 78.3 %shard_map.46 = bf16[2,4,256,256]{3,2,1,0:T(8,128)(2,1)} custom-call(bf16[2,4,256,256]{3,2,1,0:T(8,128)(2,1)} %bitcast.6, bf16[2,4,256,256]{3,2,1,0:T(8,128)(2,1)} %bitcast.7, bf16[2,4,256,256]{3,2,1,0:T(8,128)(2,1)} %bitcast.8, bf16[3,256,256]{2,1,0:T(8,128)(2,1)} %bitcast.9), custom_call_target="tpu_custom_call" | custom-call | tf_op jit(solution)/shard_map/pallas_call | solution.py:394
  78.3 2.3 %copy.6 = bf16[1,2,4,256,256]{4,3,2,1,0:T(8,128)(2,1)} copy(bf16[1,2,4,256,256]{4,3,2,1,0:T(8,128)(2,1)} %bitcast.5) | data formatting | bytes 2097152
where the time goes:
time: 80.7 us; the launch traced here: 80.6 us
  Pallas kernels  78.3 us (97%)
  local copies, waits for them, and re-layouts  2.26 us (3%)
    pallas_call x1, Pallas kernels, fused(): pl.pallas_call(functools.partial(fused_kernel, n, cells), out_shape=jax.S...  78.3 us
    unnamed x1, local copies, waits for them, and re-layouts  2.26 us

commit v1 on v0

v1 whole, which is shorter than its diff:
```python
import functools
import math

import jax
import jax.numpy as jnp
from jax import lax
from jax.experimental import pallas as pl
from jax.experimental.pallas import tpu as pltpu
from jax.sharding import PartitionSpec as P

MESH = pl.DeviceIdType.MESH
ROWS = 16
LANES = 128
QUARTERS = 4
LESSER, GREATER = 0, 1
AHEAD = 4
SHIFT = 6
LOW_LAG = 1
DONE_LAG = 2
LATE = 3
F32 = jnp.float32
BF16 = jnp.bfloat16


def nn(a, b):
    return jnp.dot(a, b, preferred_element_type=F32)


def nt(a, b):
    return lax.dot_general(a, b, (((1,), (1,)), ((), ())), preferred_element_type=F32)


def fused_kernel(
    n, cells, green_in, sig_l_in, sig_g_in, coulomb_in, out,
    green, sig_l, sig_g, coulomb, send, recv, send_p, low, pol, total,
    in_sem, coulomb_sem, sent_sem, arrive_sem, done_sem, halo_send_sem, halo_recv_sem,
):
    me = lax.axis_index("energy")
    cell = lax.axis_index("cell")
    local = green.shape[1]
    norb = green.shape[2]
    width = n // QUARTERS
    half = 2 * width
    quarter, place = me // width, lax.rem(me, width)
    home = jnp.where(quarter == 0, 1, 2)
    strip = norb // width
    row_parts = strip // ROWS
    col_parts = norb // LANES
    chunks = row_parts * col_parts
    has_low = cell > 0
    has_high = cell < cells - 1
    offset = {LESSER: 0, GREATER: n + 1}

    def load(i, e):
        source, held = ((green_in, green), (sig_g_in, sig_g), (sig_l_in, sig_l))[i]
        return pltpu.make_async_copy(source.at[:, e], held.at[:, e], in_sem.at[i, e])

    for e in range(local):
        load(0, e).start()
        load(1, e).start()

    barrier = pltpu.get_barrier_semaphore()

    def greet(other):
        pl.semaphore_signal(barrier, inc=1, device_id={"energy": other}, device_id_type=MESH)

    @pl.loop(1, width)
    def _(k):
        greet(quarter * width + lax.rem(place + k, width))

    @pl.when(quarter == 2)
    def _():
        greet(width + place)
        greet(3 * width + place)

    @pl.when(quarter == 1)
    def _():
        greet(place)

    @pl.when(quarter == 0)
    def _():
        @pl.loop(0, width)
        def _(k):
            greet(width + k)

    @pl.when(quarter != 2)
    def _():
        @pl.loop(0, width)
        def _(k):
            greet(2 * width + k)

    @pl.when(has_low)
    def _():
        pl.semaphore_signal(barrier, inc=1, device_id={"cell": cell - 1}, device_id_type=MESH)

    @pl.when(has_high)
    def _():
        pl.semaphore_signal(barrier, inc=1, device_id={"cell": cell + 1}, device_id_type=MESH)

    for e in range(local):
        load(2, e).start()
    coulomb_load = pltpu.make_async_copy(coulomb_in, coulomb, coulomb_sem)
    coulomb_load.start()

    def put(value, kind, comp, e):
        value = value.astype(BF16).reshape(width, strip, norb)
        for q in range(chunks):
            c, r = divmod(q, row_parts)
            send[kind, q, :, comp, e] = value[:, r * ROWS:(r + 1) * ROWS, c * LANES:(c + 1) * LANES]

    @pl.loop(0, local)
    def _(e):
        load(0, e).wait()
        load(1, e).wait()
        g_re, g_im = green[0, e], green[1, e]
        s_re, s_im = sig_g[0, e], sig_g[1, e]
        half_re = (nn(g_re, s_re) - nn(g_im, s_im)).astype(BF16)
        half_im = (nn(g_re, s_im) + nn(g_im, s_re)).astype(BF16)
        put(nt(g_re, half_re) + nt(g_im, half_im), GREATER, 0, e)
        put(nt(g_re, half_im) - nt(g_im, half_re), GREATER, 1, e)

    reach = jnp.where(quarter == 1, width + 1, jnp.where(quarter == 2, 3 * width, 1))
    pl.semaphore_wait(barrier, width - 1 + reach + has_low.astype(jnp.int32) + has_high.astype(jnp.int32))

    def sum_of(count):
        return recv.at[0, 0:count]

    def block_copy(source, kind, q, slot, other, lane):
        return pltpu.make_async_remote_copy(
            src_ref=source, dst_ref=recv.at[q, offset[kind] + slot],
            send_sem=sent_sem.at[q], recv_sem=arrive_sem.at[lane, q],
            device_id={"energy": other}, device_id_type=MESH,
        )

    def exchange(kind, q):
        lane = jnp.where(quarter == 2, 0, 0 if kind == GREATER else 1)

        @pl.loop(1, width)
        def _(k):
            where = lax.rem(place + k, width)
            block_copy(send.at[kind, q, where], kind, q, me, quarter * width + where, lane).start()

    def lane_at_home(kind):
        return jnp.where(quarter == 0, 2 if kind == GREATER else 1, 0)

    def forward_own(kind, q):
        block_copy(send.at[kind, q, place], kind, q, me, home * width + place, lane_at_home(kind)).start()

    def forward_others(kind, q):
        @pl.loop(1, width)
        def _(k):
            slot = quarter * width + lax.rem(place + k, width)
            block_copy(recv.at[q, offset[kind] + slot], kind, q, slot, home * width + place, lane_at_home(kind)).start()

    def arrived(lane, q, count):
        pltpu.make_async_copy(sum_of(count), sum_of(count), arrive_sem.at[lane, q]).wait()

    ahead = min(AHEAD, chunks)

    @pl.when(quarter != 2)
    def _():
        @pl.loop(0, ahead)
        def _(q):
            forward_own(GREATER, q)

    @pl.loop(0, ahead)
    def _(q):
        exchange(GREATER, q)

    @pl.loop(0, local)
    def _(e):
        load(2, e).wait()
        g_re, g_im = green[0, e], green[1, e]
        l_re, l_im = sig_l[0, e], sig_l[1, e]
        half_re = (nn(g_re, l_re) - nn(g_im, l_im)).astype(BF16)
        half_im = (nn(g_re, l_im) + nn(g_im, l_re)).astype(BF16)
        put(nt(half_re, g_re) + nt(half_im, g_im), LESSER, 0, e)
        put(nt(half_im, g_re) - nt(half_re, g_im), LESSER, 1, e)

    @pl.when(quarter == 3)
    def _():
        @pl.loop(0, ahead)
        def _(q):
            forward_own(LESSER, q)

    @pl.loop(0, ahead)
    def _(q):
        exchange(LESSER, q)

    @pl.loop(ahead, chunks)
    def _(q):
        exchange(GREATER, q)
        exchange(LESSER, q)

    blank = jnp.zeros((2, local, ROWS, LANES), BF16)

    @pl.when(jnp.logical_or(quarter == 1, quarter == 2))
    def _():
        @pl.loop(0, chunks)
        def _(q):
            for kind in (LESSER, GREATER):
                recv[q, offset[kind] + me] = send[kind, q, place]

    @pl.when(quarter == 1)
    def _():
        @pl.loop(0, chunks)
        def _(q):
            recv[q, half] = blank

    @pl.when(quarter == 2)
    def _():
        @pl.loop(0, chunks)
        def _(q):
            recv[q, half - 1] = blank
            recv[q, n] = blank

    def spot(q):
        rows = pl.ds(pl.multiple_of(lax.rem(q, row_parts) * ROWS, ROWS), ROWS)
        return rows, pl.ds(pl.multiple_of(q // row_parts * LANES, LANES), LANES)

    def return_copy(q, owner):
        return pltpu.make_async_remote_copy(
            src_ref=send_p.at[q, owner], dst_ref=pol.at[1, :, :, place, *spot(q)],
            send_sem=sent_sem.at[q], recv_sem=done_sem.at[q],
            device_id={"energy": owner}, device_id_type=MESH,
        )

    def low_copy(q, owner):
        return pltpu.make_async_remote_copy(
            src_ref=send_p.at[q, owner], dst_ref=low.at[q, place],
            send_sem=sent_sem.at[q], recv_sem=done_sem.at[q],
            device_id={"energy": owner}, device_id_type=MESH,
        )

    def halo_copy(q, slot, other):
        return pltpu.make_async_remote_copy(
            src_ref=pol.at[1, :, :, :, *spot(q)], dst_ref=pol.at[slot, :, :, :, *spot(q)],
            send_sem=halo_send_sem.at[slot // 2], recv_sem=halo_recv_sem.at[slot // 2, q // row_parts],
            device_id={"cell": other}, device_id_type=MESH,
        )

    factor = 1.0 / math.sqrt(n * local)

    def correlate(q, b, first_step, last_step):
        def step(a, acc):
            first = [
                (recv[q, a + b + i // local, 0, i % local].astype(F32), recv[q, a + b + i // local, 1, i % local].astype(F32))
                for i in range(2 * local - 1)
            ]
            acc = list(acc)
            for e in range(local):
                x_re, x_im = recv[q, n + 1 + a, 0, e].astype(F32), recv[q, n + 1 + a, 1, e].astype(F32)
                for w in range(local):
                    y_re, y_im = first[e + w]
                    acc[2 * w] = acc[2 * w] + (y_re * x_re - y_im * x_im)
                    acc[2 * w + 1] = acc[2 * w + 1] + (y_re * x_im + y_im * x_re)
            return tuple(acc)

        zero = jnp.zeros((ROWS, LANES), F32)
        acc = lax.fori_loop(first_step, last_step, step, (zero,) * (2 * local))
        for w in range(local):
            send_p[q, b, 0, w] = (acc[2 * w] * factor).astype(BF16)
            send_p[q, b, 1, w] = (acc[2 * w + 1] * factor).astype(BF16)

    def halo(q):
        @pl.when(has_low)
        def _():
            halo_copy(q, 2, cell - 1).start()

        @pl.when(has_high)
        def _():
            halo_copy(q, 0, cell + 1).start()

    def done(q, count):
        pltpu.make_async_copy(sum_of(count), sum_of(count), done_sem.at[q]).wait()

    def finish(q, count):
        done(q, count)

        @pl.loop(0, width)
        def _(where):
            for c in range(2):
                for w in range(local):
                    place_of = (1, c, w, where, *spot(q))
                    pol[place_of] = (pol[place_of].astype(F32) + low[q, where, c, w].astype(F32)).astype(BF16)

        halo(q)

    @pl.when(jnp.logical_not(has_low))
    def _():
        pol[0] = jnp.zeros_like(pol[0])

    @pl.when(jnp.logical_not(has_high))
    def _():
        pol[2] = jnp.zeros_like(pol[2])

    @pl.when(quarter == 0)
    def _():
        @pl.loop(0, chunks + SHIFT)
        def _(t):
            @pl.when(t < chunks)
            def _():
                if width > 1:
                    arrived(0, t, width - 1)
                forward_others(GREATER, t)

            @pl.when(t + ahead < chunks)
            def _():
                forward_own(GREATER, t + ahead)

            @pl.when(t >= SHIFT)
            def _():
                q = t - SHIFT
                forward_own(LESSER, q)
                if width > 1:
                    arrived(1, q, width - 1)
                forward_others(LESSER, q)

        @pl.loop(0, chunks)
        def _(q):
            finish(q, 2 * width)

    @pl.when(quarter == 1)
    def _():
        @pl.loop(0, chunks + SHIFT + LOW_LAG + DONE_LAG)
        def _(t):
            @pl.when(t < chunks)
            def _():
                if width > 1:
                    arrived(0, t, width - 1)
                forward_others(GREATER, t)
                arrived(2, t, width)
                lower = recv.at[t, n + 1:n + 1 + width]
                pltpu.make_async_remote_copy(
                    src_ref=lower, dst_ref=lower, send_sem=sent_sem.at[t], recv_sem=arrive_sem.at[0, t],
                    device_id={"energy": 2 * width + place}, device_id_type=MESH,
                ).start()

            @pl.when(t + ahead < chunks)
            def _():
                forward_own(GREATER, t + ahead)

            late = SHIFT + LOW_LAG

            @pl.when(jnp.logical_and(t >= late, t < chunks + late))
            def _():
                q = t - late
                arrived(1, q, 2 * width - 1)

                @pl.loop(0, half)
                def _(b):
                    correlate(q, b, 0, half - b)

                    @pl.when(b != me)
                    def _():
                        low_copy(q, b).start()

                    @pl.when(b == me)
                    def _():
                        low[q, place] = send_p[q, b]

            @pl.when(t >= late + DONE_LAG)
            def _():
                finish(t - late - DONE_LAG, 2 * width - 1)

    @pl.when(quarter == 2)
    def _():
        @pl.loop(0, chunks + LATE)
        def _(t):
            @pl.when(t < chunks)
            def _():
                arrived(0, t, 6 * width - 2)

                @pl.loop(0, n)
                def _(b):
                    correlate(t, b, jnp.maximum(half - 1 - b, 0), n - b)

                    @pl.when(b != me)
                    def _():
                        return_copy(t, b).start()

                    @pl.when(b == me)
                    def _():
                        pol[1, :, :, place, *spot(t)] = send_p[t, b]

            @pl.when(t >= LATE)
            def _():
                if width > 1:
                    done(t - LATE, width - 1)
                halo(t - LATE)

    @pl.when(quarter == 3)
    def _():
        @pl.loop(0, chunks)
        def _(t):
            for kind in (GREATER, LESSER):
                if width > 1:
                    arrived(0 if kind == GREATER else 1, t, width - 1)
                forward_others(kind, t)

            @pl.when(t + ahead < chunks)
            def _():
                forward_own(GREATER, t + ahead)
                forward_own(LESSER, t + ahead)

        @pl.loop(0, chunks)
        def _(q):
            done(q, width)
            halo(q)

    coulomb_load.wait()

    def polarized(slot, c, e, part):
        return pol[slot, c, e, :, :, part * LANES:(part + 1) * LANES].reshape(norb, LANES)

    @pl.loop(0, local)
    def _(e):
        for c in range(2):
            for part in range(col_parts):
                total[c, e, :, part * LANES:(part + 1) * LANES] = nn(coulomb[1], polarized(1, c, e, part))

    for part in range(col_parts):
        group = (slice(None), slice(None), slice(None), slice(None), slice(part * LANES, (part + 1) * LANES))

        @pl.when(has_low)
        def _():
            pltpu.make_async_copy(pol.at[0, *group], pol.at[0, *group], halo_recv_sem.at[0, part]).wait()

        @pl.when(has_high)
        def _():
            pltpu.make_async_copy(pol.at[2, *group], pol.at[2, *group], halo_recv_sem.at[1, part]).wait()

        @pl.loop(0, local)
        def _(e):
            for c in range(2):
                summed = total[c, e, :, part * LANES:(part + 1) * LANES]
                summed = summed + nn(coulomb[0], polarized(0, c, e, part)) + nn(coulomb[2], polarized(2, c, e, part))
                out[c, e, :, part * LANES:(part + 1) * LANES] = summed.astype(BF16)

    @pl.when(has_low)
    def _():
        pltpu.make_async_copy(pol.at[1], pol.at[1], halo_send_sem.at[1]).wait()

    @pl.when(has_high)
    def _():
        pltpu.make_async_copy(pol.at[1], pol.at[1], halo_send_sem.at[0]).wait()

    def all_sent(count):
        @pl.loop(0, chunks)
        def _(q):
            pltpu.make_async_copy(sum_of(count), sum_of(count), sent_sem.at[q]).wait()

    @pl.when(jnp.logical_or(quarter == 0, quarter == 3))
    def _():
        all_sent(4 * width - 2)

    @pl.when(jnp.logical_or(quarter == 1, quarter == 2))
    def _():
        all_sent(6 * width - 3)


def fused(n, cells, retarded, sigma_lesser, sigma_greater, coulomb):
    green = retarded[0]
    local, norb = green.shape[1], green.shape[2]
    width = n // QUARTERS
    strip = norb // width
    chunks = strip // ROWS * (norb // LANES)
    dma = pltpu.SemaphoreType.DMA
    result = pl.pallas_call(
        functools.partial(fused_kernel, n, cells),
        out_shape=pltpu.VMEM(green.shape, BF16),
        in_specs=[pl.BlockSpec(memory_space=pltpu.HBM)] * 4,
        out_specs=pl.BlockSpec(memory_space=pltpu.VMEM),
        scratch_shapes=[
            pltpu.VMEM(green.shape, BF16),
            pltpu.VMEM(green.shape, BF16),
            pltpu.VMEM(green.shape, BF16),
            pltpu.VMEM(coulomb.shape[1:], BF16),
            pltpu.VMEM((2, chunks, width, 2, local, ROWS, LANES), BF16),
            pltpu.VMEM((chunks, 2 * n + 1, 2, local, ROWS, LANES), BF16),
            pltpu.VMEM((chunks, n, 2, local, ROWS, LANES), BF16),
            pltpu.VMEM((chunks, width, 2, local, ROWS, LANES), BF16),
            pltpu.VMEM((3, 2, local, width, strip, norb), BF16),
            pltpu.VMEM((2, local, norb, norb), F32),
            dma((3, local)), dma,
            dma((chunks,)), dma((3, chunks)), dma((chunks,)),
            dma((2,)), dma((2, norb // LANES)),
        ],
        compiler_params=pltpu.CompilerParams(
            collective_id=0, has_side_effects=True, vmem_limit_bytes=56 * 1024 * 1024
        ),
    )(green, sigma_lesser[0], sigma_greater[0], coulomb[0])
    return result[None]


def thin(n, cells, retarded, sigma_lesser, sigma_greater, coulomb):
    green = retarded[0]
    local = green.shape[1]

    def halves(sigma):
        def product(x, y):
            return jnp.einsum("eik,ekj->eij", x, y, preferred_element_type=F32)

        re = product(green[0], sigma[0]) - product(green[1], sigma[1])
        im = product(green[0], sigma[1]) + product(green[1], sigma[0])
        return re.astype(BF16), im.astype(BF16)

    def adjoint(x, y):
        return jnp.einsum("eik,ejk->eij", x, y, preferred_element_type=F32)

    re, im = halves(sigma_lesser[0])
    lesser = jnp.stack([adjoint(re, green[0]) + adjoint(im, green[1]), adjoint(im, green[0]) - adjoint(re, green[1])])
    re, im = halves(sigma_greater[0])
    greater = jnp.stack([adjoint(green[0], re) + adjoint(green[1], im), adjoint(green[0], im) - adjoint(green[1], re)])
    first = lax.all_to_all(lesser.astype(BF16), "energy", split_axis=2, concat_axis=1, tiled=True).astype(F32)
    second = lax.all_to_all(greater.astype(BF16), "energy", split_axis=2, concat_axis=1, tiled=True).astype(F32)
    energies = n * local
    padded = jnp.concatenate([first, jnp.zeros_like(first)], axis=1)

    def lag(w):
        y = lax.dynamic_slice_in_dim(padded, w, energies, axis=1)
        re = jnp.sum(y[0] * second[0] - y[1] * second[1], axis=0)
        im = jnp.sum(y[0] * second[1] + y[1] * second[0], axis=0)
        return (jnp.stack([re, im]) / math.sqrt(energies)).astype(BF16)

    polarized = jnp.swapaxes(lax.map(lag, jnp.arange(energies)), 0, 1)
    polarized = lax.all_to_all(polarized, "energy", split_axis=1, concat_axis=2, tiled=True)
    up = [(i, i + 1) for i in range(cells - 1)]
    low = lax.ppermute(polarized, "cell", up)
    high = lax.ppermute(polarized, "cell", [(t, s) for s, t in up])
    stacked = jnp.stack([low, polarized, high])
    summed = jnp.einsum("dik,dcekj->ceij", coulomb[0], stacked, preferred_element_type=F32)
    return summed.astype(BF16)[None]


def solution(mesh):
    n, cells = mesh.shape["energy"], mesh.shape["cell"]

    def on_device(retarded, sigma_lesser, sigma_greater, coulomb):
        norb = retarded.shape[-1]
        whole_tiles = n % QUARTERS == 0 and norb % LANES == 0 and norb % (n // QUARTERS * ROWS) == 0
        plan = fused if whole_tiles else thin
        return plan(n, cells, retarded, sigma_lesser, sigma_greater, coulomb)

    in_specs = (
        P("cell", None, "energy", None, None),
        P("cell", None, "energy", None, None),
        P("cell", None, "energy", None, None),
        P("cell", None, None, None),
    )
    out_specs = P("cell", None, "energy", None, None)
    return jax.shard_map(
        on_device, mesh=mesh, in_specs=in_specs, out_specs=out_specs, check_vma=False
    )
```

time: 80.7 us -> 75.9 us (0.941)
  Pallas kernels: 78.3 us -> 74.8 us
  local copies, waits for them, and re-layouts: 2.26 us -> 0.97 us
    pallas_call x1, Pallas kernels: 78.3 us -> 74.8 us  [fused(): pl.pallas_call(functools.partial(fused_kernel, n, cells), out_shape=pltpu...]
    unnamed x1, local copies, waits for them, and re-layouts: 2.26 us -> 0.97 us
where the time goes in v1:
time: 75.9 us; the launch traced here: 75.8 us
  Pallas kernels  74.8 us (99%)
  local copies, waits for them, and re-layouts  0.97 us (1%)
    pallas_call x1, Pallas kernels, fused(): pl.pallas_call(functools.partial(fused_kernel, n, cells), out_shape=pltpu...  74.8 us

profile of v1, /device:TPU:1, one launch (start us, length us, event | category | flops | bytes accessed | tf_op | source)
XLA Modules:
  0.0 75.8 jit_solution(14476796910777094190)
XLA Ops:
  0.0 74.8 %shard_map.46 = bf16[2,4,256,256]{3,2,1,0:T(8,128)(2,1)S(1)} custom-call(bf16[2,4,256,256]{3,2,1,0:T(8,128)(2,1)} %bitcast.6, bf16[2,4,256,256]{3,2,1,0:T(8,128)(2,1)} %bitcast.7, bf16[2,4,256,256]{3,2,1,0:T(8,128)(2,1)} %bitcast.8, bf16[3,256,256]{2,1,0:T(8,128)(2,1)} %bitcast.9), custom_call_target="tpu_custom_call" | custom-call | tf_op jit(solution)/shard_map/pallas_call | solution.py:469
  74.8 1.0 %copy.6 = bf16[1,2,4,256,256]{4,3,2,1,0:T(8,128)(2,1)} copy(bf16[1,2,4,256,256]{4,3,2,1,0:T(8,128)(2,1)S(1)} %bitcast.5) | data formatting | bytes 2097152

commit v2 on v1

--- a/solution.py
+++ b/solution.py
@@ -13,10 +13,13 @@
 LANES = 128
 QUARTERS = 4
 LESSER, GREATER = 0, 1
+DIRECT = 1
 AHEAD = 4
-SHIFT = 6
-LOW_LAG = 1
-DONE_LAG = 2
+AHEAD_TOP = 2
+EARLY = 4
+SHIFT = 1
+LOW_LAG = 0
+DONE_LAG = 6
 LATE = 3
 F32 = jnp.float32
 BF16 = jnp.bfloat16
@@ -47,10 +50,14 @@
     row_parts = strip // ROWS
     col_parts = norb // LANES
     chunks = row_parts * col_parts
+    straight = min(DIRECT, chunks)
     has_low = cell > 0
     has_high = cell < cells - 1
     offset = {LESSER: 0, GREATER: n + 1}
 
+    def batch(q):
+        return jnp.where(q < straight, 0, 1)
+
     def load(i, e):
         source, held = ((green_in, green), (sig_g_in, sig_g), (sig_l_in, sig_l))[i]
         return pltpu.make_async_copy(source.at[:, e], held.at[:, e], in_sem.at[i, e])
@@ -68,26 +75,16 @@
     def _(k):
         greet(quarter * width + lax.rem(place + k, width))
 
-    @pl.when(quarter == 2)
-    def _():
-        greet(width + place)
-        greet(3 * width + place)
-
-    @pl.when(quarter == 1)
-    def _():
-        greet(place)
-
-    @pl.when(quarter == 0)
-    def _():
+    def greet_quarter(other):
         @pl.loop(0, width)
         def _(k):
-            greet(width + k)
-
-    @pl.when(quarter != 2)
-    def _():
-        @pl.loop(0, width)
-        def _(k):
-            greet(2 * width + k)
+            greet(other * width + k)
+
+    for mine, others in ((0, (1, 2)), (1, (0, 2)), (2, (1, 3)), (3, (2,))):
+        @pl.when(quarter == mine)
+        def _():
+            for other in others:
+                greet_quarter(other)
 
     @pl.when(has_low)
     def _():
@@ -114,12 +111,13 @@
         load(1, e).wait()
         g_re, g_im = green[0, e], green[1, e]
         s_re, s_im = sig_g[0, e], sig_g[1, e]
-        half_re = (nn(g_re, s_re) - nn(g_im, s_im)).astype(BF16)
+        g_neg = -g_im
+        half_re = (nn(g_re, s_re) + nn(g_neg, s_im)).astype(BF16)
         half_im = (nn(g_re, s_im) + nn(g_im, s_re)).astype(BF16)
         put(nt(g_re, half_re) + nt(g_im, half_im), GREATER, 0, e)
-        put(nt(g_re, half_im) - nt(g_im, half_re), GREATER, 1, e)
-
-    reach = jnp.where(quarter == 1, width + 1, jnp.where(quarter == 2, 3 * width, 1))
+        put(nt(g_re, half_im) + nt(g_neg, half_re), GREATER, 1, e)
+
+    reach = width * jnp.where(quarter == 1, 2, jnp.where(quarter == 2, 3, 1))
     pl.semaphore_wait(barrier, width - 1 + reach + has_low.astype(jnp.int32) + has_high.astype(jnp.int32))
 
     def sum_of(count):
@@ -128,7 +126,7 @@
     def block_copy(source, kind, q, slot, other, lane):
         return pltpu.make_async_remote_copy(
             src_ref=source, dst_ref=recv.at[q, offset[kind] + slot],
-            send_sem=sent_sem.at[q], recv_sem=arrive_sem.at[lane, q],
+            send_sem=sent_sem.at[batch(q)], recv_sem=arrive_sem.at[lane, q],
             device_id={"energy": other}, device_id_type=MESH,
         )
 
@@ -155,15 +153,27 @@
     def arrived(lane, q, count):
         pltpu.make_async_copy(sum_of(count), sum_of(count), arrive_sem.at[lane, q]).wait()
 
-    ahead = min(AHEAD, chunks)
+    def direct(kind, q):
+        @pl.loop(0, width)
+        def _(where):
+            block_copy(send.at[kind, q, where], kind, q, me, home * width + where, lane_at_home(kind)).start()
+
+    ahead = jnp.where(quarter == 3, min(AHEAD_TOP, chunks), min(AHEAD, chunks))
+    first = jnp.where(quarter == 3, straight, 0)
+
+    @pl.when(jnp.logical_or(quarter == 1, quarter == 3))
+    def _():
+        @pl.loop(0, straight)
+        def _(q):
+            direct(GREATER, q)
 
     @pl.when(quarter != 2)
     def _():
-        @pl.loop(0, ahead)
+        @pl.loop(jnp.where(quarter == 0, 0, straight), ahead)
         def _(q):
             forward_own(GREATER, q)
 
-    @pl.loop(0, ahead)
+    @pl.loop(first, ahead)
     def _(q):
         exchange(GREATER, q)
 
@@ -172,26 +182,37 @@
         load(2, e).wait()
         g_re, g_im = green[0, e], green[1, e]
         l_re, l_im = sig_l[0, e], sig_l[1, e]
-        half_re = (nn(g_re, l_re) - nn(g_im, l_im)).astype(BF16)
+        g_neg = -g_im
+        half_re = (nn(g_re, l_re) + nn(g_neg, l_im)).astype(BF16)
         half_im = (nn(g_re, l_im) + nn(g_im, l_re)).astype(BF16)
         put(nt(half_re, g_re) + nt(half_im, g_im), LESSER, 0, e)
-        put(nt(half_im, g_re) - nt(half_re, g_im), LESSER, 1, e)
+        put(nt(half_im, g_re) + nt(half_re, g_neg), LESSER, 1, e)
 
     @pl.when(quarter == 3)
     def _():
-        @pl.loop(0, ahead)
+        @pl.loop(0, straight)
+        def _(q):
+            direct(LESSER, q)
+
+        @pl.loop(straight, ahead)
         def _(q):
             forward_own(LESSER, q)
 
-    @pl.loop(0, ahead)
+    @pl.loop(first, ahead)
     def _(q):
         exchange(LESSER, q)
 
-    @pl.loop(ahead, chunks)
+    @pl.loop(ahead, jnp.where(jnp.logical_or(quarter == 1, quarter == 2), min(EARLY, chunks), chunks))
     def _(q):
         exchange(GREATER, q)
         exchange(LESSER, q)
 
+    def more(t):
+        @pl.when(t + EARLY < chunks)
+        def _():
+            exchange(GREATER, t + EARLY)
+            exchange(LESSER, t + EARLY)
+
     blank = jnp.zeros((2, local, ROWS, LANES), BF16)
 
     @pl.when(jnp.logical_or(quarter == 1, quarter == 2))
@@ -221,14 +242,14 @@
     def return_copy(q, owner):
         return pltpu.make_async_remote_copy(
             src_ref=send_p.at[q, owner], dst_ref=pol.at[1, :, :, place, *spot(q)],
-            send_sem=sent_sem.at[q], recv_sem=done_sem.at[q],
+            send_sem=sent_sem.at[batch(q)], recv_sem=done_sem.at[q],
             device_id={"energy": owner}, device_id_type=MESH,
         )
 
     def low_copy(q, owner):
         return pltpu.make_async_remote_copy(
             src_ref=send_p.at[q, owner], dst_ref=low.at[q, place],
-            send_sem=sent_sem.at[q], recv_sem=done_sem.at[q],
+            send_sem=sent_sem.at[batch(q)], recv_sem=done_sem.at[q],
             device_id={"energy": owner}, device_id_type=MESH,
         )
 
@@ -328,13 +349,18 @@
             def _():
                 if width > 1:
                     arrived(0, t, width - 1)
-                forward_others(GREATER, t)
+
+                @pl.when(t >= straight)
+                def _():
+                    forward_others(GREATER, t)
+
                 arrived(2, t, width)
                 lower = recv.at[t, n + 1:n + 1 + width]
                 pltpu.make_async_remote_copy(
-                    src_ref=lower, dst_ref=lower, send_sem=sent_sem.at[t], recv_sem=arrive_sem.at[0, t],
+                    src_ref=lower, dst_ref=lower, send_sem=sent_sem.at[batch(t)], recv_sem=arrive_sem.at[0, t],
                     device_id={"energy": 2 * width + place}, device_id_type=MESH,
                 ).start()
+                more(t)
 
             @pl.when(t + ahead < chunks)
             def _():
@@ -370,6 +396,7 @@
             @pl.when(t < chunks)
             def _():
                 arrived(0, t, 6 * width - 2)
+                more(t)
 
                 @pl.loop(0, n)
                 def _(b):
@@ -391,17 +418,17 @@
 
     @pl.when(quarter == 3)
     def _():
-        @pl.loop(0, chunks)
+        @pl.loop(straight, chunks)
         def _(t):
             for kind in (GREATER, LESSER):
                 if width > 1:
                     arrived(0 if kind == GREATER else 1, t, width - 1)
                 forward_others(kind, t)
 
-            @pl.when(t + ahead < chunks)
-            def _():
-                forward_own(GREATER, t + ahead)
-                forward_own(LESSER, t + ahead)
+            @pl.when(t + ahead - straight < chunks)
+            def _():
+                forward_own(GREATER, t + ahead - straight)
+                forward_own(LESSER, t + ahead - straight)
 
         @pl.loop(0, chunks)
         def _(q):
@@ -410,17 +437,19 @@
 
     coulomb_load.wait()
 
-    def polarized(slot, c, e, part):
-        return pol[slot, c, e, :, :, part * LANES:(part + 1) * LANES].reshape(norb, LANES)
+    def polarized(slot, e, part):
+        cols = slice(part * LANES, (part + 1) * LANES)
+        return jnp.concatenate([pol[slot, c, e, :, :, cols].reshape(norb, LANES) for c in range(2)], 1)
+
+    last = col_parts - 1
 
     @pl.loop(0, local)
     def _(e):
-        for c in range(2):
-            for part in range(col_parts):
-                total[c, e, :, part * LANES:(part + 1) * LANES] = nn(coulomb[1], polarized(1, c, e, part))
+        total[e] = nn(coulomb[1], polarized(1, e, last))
 
     for part in range(col_parts):
-        group = (slice(None), slice(None), slice(None), slice(None), slice(part * LANES, (part + 1) * LANES))
+        cols = slice(part * LANES, (part + 1) * LANES)
+        group = (slice(None), slice(None), slice(None), slice(None), cols)
 
         @pl.when(has_low)
         def _():
@@ -432,10 +461,10 @@
 
         @pl.loop(0, local)
         def _(e):
+            middle = total[e] if part == last else nn(coulomb[1], polarized(1, e, part))
+            summed = nn(coulomb[0], polarized(0, e, part)) + nn(coulomb[2], polarized(2, e, part)) + middle
             for c in range(2):
-                summed = total[c, e, :, part * LANES:(part + 1) * LANES]
-                summed = summed + nn(coulomb[0], polarized(0, c, e, part)) + nn(coulomb[2], polarized(2, c, e, part))
-                out[c, e, :, part * LANES:(part + 1) * LANES] = summed.astype(BF16)
+                out[c, e, :, cols] = summed[:, c * LANES:(c + 1) * LANES].astype(BF16)
 
     @pl.when(has_low)
     def _():
@@ -445,18 +474,23 @@
     def _():
         pltpu.make_async_copy(pol.at[1], pol.at[1], halo_send_sem.at[0]).wait()
 
-    def all_sent(count):
-        @pl.loop(0, chunks)
-        def _(q):
-            pltpu.make_async_copy(sum_of(count), sum_of(count), sent_sem.at[q]).wait()
-
-    @pl.when(jnp.logical_or(quarter == 0, quarter == 3))
-    def _():
-        all_sent(4 * width - 2)
+    def all_sent(*counts):
+        for i, (count, size) in enumerate(zip(counts, (straight, chunks - straight))):
+            if count * size:
+                sent = recv.at[0:size, 0:count]
+                pltpu.make_async_copy(sent, sent, sent_sem.at[i]).wait()
+
+    @pl.when(quarter == 0)
+    def _():
+        all_sent(4 * width - 2, 4 * width - 2)
+
+    @pl.when(quarter == 3)
+    def _():
+        all_sent(2 * width, 4 * width - 2)
 
     @pl.when(jnp.logical_or(quarter == 1, quarter == 2))
     def _():
-        all_sent(6 * width - 3)
+        all_sent(6 * width - 3, 6 * width - 3)
 
 
 def fused(n, cells, retarded, sigma_lesser, sigma_greater, coulomb):
@@ -481,9 +515,9 @@
             pltpu.VMEM((chunks, n, 2, local, ROWS, LANES), BF16),
             pltpu.VMEM((chunks, width, 2, local, ROWS, LANES), BF16),
             pltpu.VMEM((3, 2, local, width, strip, norb), BF16),
-            pltpu.VMEM((2, local, norb, norb), F32),
+            pltpu.VMEM((local, norb, 2 * LANES), F32),
             dma((3, local)), dma,
-            dma((chunks,)), dma((3, chunks)), dma((chunks,)),
+            dma((2,)), dma((3, chunks)), dma((chunks,)),
             dma((2,)), dma((2, norb // LANES)),
         ],
         compiler_params=pltpu.CompilerParams(

time: 75.9 us -> 67.2 us (0.89)
  Pallas kernels: 74.8 us -> 66.1 us
    pallas_call x1, Pallas kernels: 74.8 us -> 66.1 us  [fused(): pl.pallas_call(functools.partial(fused_kernel, n, cells), out_shape=pltpu...]
where the time goes in v2:
time: 67.2 us; the launch traced here: 67 us
  Pallas kernels  66.1 us (98%)
  local copies, waits for them, and re-layouts  0.97 us (1%)
    pallas_call x1, Pallas kernels, fused(): pl.pallas_call(functools.partial(fused_kernel, n, cells), out_shape=pltpu...  66.1 us

profile of v2, /device:TPU:1, one launch (start us, length us, event | category | flops | bytes accessed | tf_op | source)
XLA Modules:
  0.0 67.0 jit_solution(7376049728450806735)
XLA Ops:
  0.0 66.1 %shard_map.46 = bf16[2,4,256,256]{3,2,1,0:T(8,128)(2,1)S(1)} custom-call(bf16[2,4,256,256]{3,2,1,0:T(8,128)(2,1)} %bitcast.6, bf16[2,4,256,256]{3,2,1,0:T(8,128)(2,1)} %bitcast.7, bf16[2,4,256,256]{3,2,1,0:T(8,128)(2,1)} %bitcast.8, bf16[3,256,256]{2,1,0:T(8,128)(2,1)} %bitcast.9), custom_call_target="tpu_custom_call" | custom-call | tf_op jit(solution)/shard_map/pallas_call | solution.py:503
  66.1 1.0 %copy.6 = bf16[1,2,4,256,256]{4,3,2,1,0:T(8,128)(2,1)} copy(bf16[1,2,4,256,256]{4,3,2,1,0:T(8,128)(2,1)S(1)} %bitcast.5) | data formatting | bytes 2097152

commit v3 on v2

--- a/solution.py
+++ b/solution.py
@@ -14,7 +14,7 @@
 QUARTERS = 4
 LESSER, GREATER = 0, 1
 DIRECT = 1
-AHEAD = 4
+AHEAD = 3
 AHEAD_TOP = 2
 EARLY = 4
 SHIFT = 1
@@ -105,6 +105,23 @@
             c, r = divmod(q, row_parts)
             send[kind, q, :, comp, e] = value[:, r * ROWS:(r + 1) * ROWS, c * LANES:(c + 1) * LANES]
 
+    reach = width * jnp.where(quarter == 1, 2, jnp.where(quarter == 2, 3, 1))
+
+    def meet():
+        pl.semaphore_wait(barrier, width - 1 + reach + has_low.astype(jnp.int32) + has_high.astype(jnp.int32))
+
+    pl.when(quarter == 3)(meet)
+
+    def sum_of(count):
+        return recv.at[0, 0:count]
+
+    def block_copy(source, kind, q, slot, other, lane):
+        return pltpu.make_async_remote_copy(
+            src_ref=source, dst_ref=recv.at[q, offset[kind] + slot],
+            send_sem=sent_sem.at[batch(q)], recv_sem=arrive_sem.at[lane, q],
+            device_id={"energy": other}, device_id_type=MESH,
+        )
+
     @pl.loop(0, local)
     def _(e):
         load(0, e).wait()
@@ -117,18 +134,19 @@
         put(nt(g_re, half_re) + nt(g_im, half_im), GREATER, 0, e)
         put(nt(g_re, half_im) + nt(g_neg, half_re), GREATER, 1, e)
 
-    reach = width * jnp.where(quarter == 1, 2, jnp.where(quarter == 2, 3, 1))
-    pl.semaphore_wait(barrier, width - 1 + reach + has_low.astype(jnp.int32) + has_high.astype(jnp.int32))
-
-    def sum_of(count):
-        return recv.at[0, 0:count]
-
-    def block_copy(source, kind, q, slot, other, lane):
-        return pltpu.make_async_remote_copy(
-            src_ref=source, dst_ref=recv.at[q, offset[kind] + slot],
-            send_sem=sent_sem.at[batch(q)], recv_sem=arrive_sem.at[lane, q],
-            device_id={"energy": other}, device_id_type=MESH,
-        )
+        @pl.when(quarter == 3)
+        def _():
+            for q in range(straight):
+                @pl.loop(0, width)
+                def _(where):
+                    pltpu.make_async_remote_copy(
+                        src_ref=send.at[GREATER, q, where, :, e], dst_ref=recv.at[q, offset[GREATER] + me, :, e],
+                        send_sem=sent_sem.at[batch(q)], recv_sem=arrive_sem.at[0, q],
+                        device_id={"energy": home * width + where}, device_id_type=MESH,
+                    ).start()
+
+    pl.when(quarter != 3)(meet)
+
 
     def exchange(kind, q):
         lane = jnp.where(quarter == 2, 0, 0 if kind == GREATER else 1)
@@ -161,7 +179,7 @@
     ahead = jnp.where(quarter == 3, min(AHEAD_TOP, chunks), min(AHEAD, chunks))
     first = jnp.where(quarter == 3, straight, 0)
 
-    @pl.when(jnp.logical_or(quarter == 1, quarter == 3))
+    @pl.when(quarter == 1)
     def _():
         @pl.loop(0, straight)
         def _(q):

time: 67.2 us -> 66.7 us (level)
  no operation moved by 1% of the time
where the time goes in v3:
time: 66.7 us; the launch traced here: 66.6 us
  Pallas kernels  65.6 us (98%)
  local copies, waits for them, and re-layouts  0.97 us (1%)
    pallas_call x1, Pallas kernels, fused(): pl.pallas_call(functools.partial(fused_kernel, n, cells), out_shape=pltpu...  65.6 us

profile of v3, /device:TPU:1, one launch (start us, length us, event | category | flops | bytes accessed | tf_op | source)
XLA Modules:
  0.0 66.6 jit_solution(12473422285438104611)
XLA Ops:
  0.0 65.6 %shard_map.46 = bf16[2,4,256,256]{3,2,1,0:T(8,128)(2,1)S(1)} custom-call(bf16[2,4,256,256]{3,2,1,0:T(8,128)(2,1)} %bitcast.6, bf16[2,4,256,256]{3,2,1,0:T(8,128)(2,1)} %bitcast.7, bf16[2,4,256,256]{3,2,1,0:T(8,128)(2,1)} %bitcast.8, bf16[3,256,256]{2,1,0:T(8,128)(2,1)} %bitcast.9), custom_call_target="tpu_custom_call" | custom-call | tf_op jit(solution)/shard_map/pallas_call | solution.py:521
  65.6 1.0 %copy.6 = bf16[1,2,4,256,256]{4,3,2,1,0:T(8,128)(2,1)} copy(bf16[1,2,4,256,256]{4,3,2,1,0:T(8,128)(2,1)S(1)} %bitcast.5) | data formatting | bytes 2097152

commit v4 on v3

--- a/solution.py
+++ b/solution.py
@@ -17,8 +17,7 @@
 AHEAD = 3
 AHEAD_TOP = 2
 EARLY = 4
-SHIFT = 1
-LOW_LAG = 0
+LOW_LAG = 8
 DONE_LAG = 6
 LATE = 3
 F32 = jnp.float32
@@ -35,7 +34,7 @@
 
 def fused_kernel(
     n, cells, green_in, sig_l_in, sig_g_in, coulomb_in, out,
-    green, sig_l, sig_g, coulomb, send, recv, send_p, low, pol, total,
+    green, sig_l, sig_g, coulomb, send, recv, send_p, low, part, pol, total,
     in_sem, coulomb_sem, sent_sem, arrive_sem, done_sem, halo_send_sem, halo_recv_sem,
 ):
     me = lax.axis_index("energy")
@@ -233,7 +232,7 @@
 
     blank = jnp.zeros((2, local, ROWS, LANES), BF16)
 
-    @pl.when(jnp.logical_or(quarter == 1, quarter == 2))
+    @pl.when(quarter != 3)
     def _():
         @pl.loop(0, chunks)
         def _(q):
@@ -244,7 +243,14 @@
     def _():
         @pl.loop(0, chunks)
         def _(q):
+            recv[q, width - 1] = blank
             recv[q, half] = blank
+
+    @pl.when(quarter == 0)
+    def _():
+        @pl.loop(0, chunks)
+        def _(q):
+            recv[q, width] = blank
 
     @pl.when(quarter == 2)
     def _():
@@ -280,7 +286,7 @@
 
     factor = 1.0 / math.sqrt(n * local)
 
-    def correlate(q, b, first_step, last_step):
+    def correlate(q, b, first_step, last_step, extra=None):
         def step(a, acc):
             first = [
                 (recv[q, a + b + i // local, 0, i % local].astype(F32), recv[q, a + b + i // local, 1, i % local].astype(F32))
@@ -298,8 +304,11 @@
         zero = jnp.zeros((ROWS, LANES), F32)
         acc = lax.fori_loop(first_step, last_step, step, (zero,) * (2 * local))
         for w in range(local):
-            send_p[q, b, 0, w] = (acc[2 * w] * factor).astype(BF16)
-            send_p[q, b, 1, w] = (acc[2 * w + 1] * factor).astype(BF16)
+            for c in range(2):
+                value = acc[2 * w + c] * factor
+                if extra is not None:
+                    value = value + extra[q, b, c, w].astype(F32)
+                send_p[q, b, c, w] = value.astype(BF16)
 
     def halo(q):
         @pl.when(has_low)
@@ -333,35 +342,54 @@
     def _():
         pol[2] = jnp.zeros_like(pol[2])
 
+    def low_out(q, b):
+        @pl.when(b != me)
+        def _():
+            low_copy(q, b).start()
+
+        @pl.when(b == me)
+        def _():
+            low[q, place] = send_p[q, b]
+
+    def part_copy(q, b):
+        return pltpu.make_async_remote_copy(
+            src_ref=send_p.at[q, b], dst_ref=part.at[q, b],
+            send_sem=sent_sem.at[batch(q)], recv_sem=arrive_sem.at[2, q],
+            device_id={"energy": place}, device_id_type=MESH,
+        )
+
     @pl.when(quarter == 0)
     def _():
-        @pl.loop(0, chunks + SHIFT)
+        @pl.loop(0, chunks)
+        def _(t):
+            if width > 1:
+                arrived(0, t, width - 1)
+            forward_others(GREATER, t)
+
+            @pl.when(t + ahead < chunks)
+            def _():
+                forward_own(GREATER, t + ahead)
+
+        @pl.loop(0, chunks + LOW_LAG)
         def _(t):
             @pl.when(t < chunks)
             def _():
                 if width > 1:
-                    arrived(0, t, width - 1)
-                forward_others(GREATER, t)
-
-            @pl.when(t + ahead < chunks)
-            def _():
-                forward_own(GREATER, t + ahead)
-
-            @pl.when(t >= SHIFT)
-            def _():
-                q = t - SHIFT
-                forward_own(LESSER, q)
-                if width > 1:
-                    arrived(1, q, width - 1)
-                forward_others(LESSER, q)
-
-        @pl.loop(0, chunks)
-        def _(q):
-            finish(q, 2 * width)
+                    arrived(1, t, width - 1)
+                arrived(2, t, width)
+
+                @pl.loop(0, width)
+                def _(b):
+                    correlate(t, b, 0, width - b, part)
+                    low_out(t, b)
+
+            @pl.when(t >= LOW_LAG)
+            def _():
+                finish(t - LOW_LAG, 2 * width - 1)
 
     @pl.when(quarter == 1)
     def _():
-        @pl.loop(0, chunks + SHIFT + LOW_LAG + DONE_LAG)
+        @pl.loop(0, chunks + DONE_LAG)
         def _(t):
             @pl.when(t < chunks)
             def _():
@@ -384,28 +412,26 @@
             def _():
                 forward_own(GREATER, t + ahead)
 
-            late = SHIFT + LOW_LAG
-
-            @pl.when(jnp.logical_and(t >= late, t < chunks + late))
-            def _():
-                q = t - late
-                arrived(1, q, 2 * width - 1)
+            @pl.when(t < chunks)
+            def _():
+                if width > 1:
+                    arrived(1, t, width - 1)
 
                 @pl.loop(0, half)
                 def _(b):
-                    correlate(q, b, 0, half - b)
-
-                    @pl.when(b != me)
+                    correlate(t, b, jnp.maximum(width - 1 - b, 0), half - b)
+
+                    @pl.when(b < width)
                     def _():
-                        low_copy(q, b).start()
-
-                    @pl.when(b == me)
+                        part_copy(t, b).start()
+
+                    @pl.when(b >= width)
                     def _():
-                        low[q, place] = send_p[q, b]
-
-            @pl.when(t >= late + DONE_LAG)
-            def _():
-                finish(t - late - DONE_LAG, 2 * width - 1)
+                        low_out(t, b)
+
+            @pl.when(t >= DONE_LAG)
+            def _():
+                finish(t - DONE_LAG, 2 * width - 1)
 
     @pl.when(quarter == 2)
     def _():
@@ -500,7 +526,7 @@
 
     @pl.when(quarter == 0)
     def _():
-        all_sent(4 * width - 2, 4 * width - 2)
+        all_sent(4 * width - 3, 4 * width - 3)
 
     @pl.when(quarter == 3)
     def _():
@@ -532,6 +558,7 @@
             pltpu.VMEM((chunks, 2 * n + 1, 2, local, ROWS, LANES), BF16),
             pltpu.VMEM((chunks, n, 2, local, ROWS, LANES), BF16),
             pltpu.VMEM((chunks, width, 2, local, ROWS, LANES), BF16),
+            pltpu.VMEM((chunks, width, 2, local, ROWS, LANES), BF16),
             pltpu.VMEM((3, 2, local, width, strip, norb), BF16),
             pltpu.VMEM((local, norb, 2 * LANES), F32),
             dma((3, local)), dma,

time: 66.7 us -> 66.1 us (level)
  no operation moved by 1% of the time
where the time goes in v4:
time: 66.1 us; the launch traced here: 65.9 us
  Pallas kernels  65 us (98%)
  local copies, waits for them, and re-layouts  0.97 us (1%)
    pallas_call x1, Pallas kernels, fused(): pl.pallas_call(functools.partial(fused_kernel, n, cells), out_shape=pltpu...  65 us

profile of v4, /device:TPU:1, one launch (start us, length us, event | category | flops | bytes accessed | tf_op | source)
XLA Modules:
  0.0 65.9 jit_solution(14515688098024931878)
XLA Ops:
  0.0 65.0 %shard_map.46 = bf16[2,4,256,256]{3,2,1,0:T(8,128)(2,1)S(1)} custom-call(bf16[2,4,256,256]{3,2,1,0:T(8,128)(2,1)} %bitcast.6, bf16[2,4,256,256]{3,2,1,0:T(8,128)(2,1)} %bitcast.7, bf16[2,4,256,256]{3,2,1,0:T(8,128)(2,1)} %bitcast.8, bf16[3,256,256]{2,1,0:T(8,128)(2,1)} %bitcast.9), custom_call_target="tpu_custom_call" | custom-call | tf_op jit(solution)/shard_map/pallas_call | solution.py:547
  65.0 1.0 %copy.6 = bf16[1,2,4,256,256]{4,3,2,1,0:T(8,128)(2,1)} copy(bf16[1,2,4,256,256]{4,3,2,1,0:T(8,128)(2,1)S(1)} %bitcast.5) | data formatting | bytes 2097152

commit v5 on v4

--- a/solution.py
+++ b/solution.py
@@ -491,22 +491,33 @@
     def _(e):
         total[e] = nn(coulomb[1], polarized(1, e, last))
 
-    for part in range(col_parts):
-        cols = slice(part * LANES, (part + 1) * LANES)
-        group = (slice(None), slice(None), slice(None), slice(None), cols)
-
-        @pl.when(has_low)
-        def _():
-            pltpu.make_async_copy(pol.at[0, *group], pol.at[0, *group], halo_recv_sem.at[0, part]).wait()
-
-        @pl.when(has_high)
-        def _():
-            pltpu.make_async_copy(pol.at[2, *group], pol.at[2, *group], halo_recv_sem.at[1, part]).wait()
+    near = jnp.where(lax.rem(cell, 2) == 0, 2, 0)
+
+    def halo_arrived(slot, part):
+        group = (slice(None), slice(None), slice(None), slice(None), slice(part * LANES, (part + 1) * LANES))
+
+        @pl.when(jnp.where(slot == 0, cell, cells - 1 - cell) > 0)
+        def _():
+            pltpu.make_async_copy(pol.at[slot, *group], pol.at[slot, *group], halo_recv_sem.at[slot // 2, part]).wait()
+
+    for part_of in range(col_parts):
+        cols = slice(part_of * LANES, (part_of + 1) * LANES)
+        halo_arrived(near, part_of)
+
+        if part_of == last:
+            @pl.loop(0, local)
+            def _(e):
+                total[e] = total[e] + nn(coulomb[near], polarized(near, e, part_of))
+
+        halo_arrived(2 - near, part_of)
 
         @pl.loop(0, local)
         def _(e):
-            middle = total[e] if part == last else nn(coulomb[1], polarized(1, e, part))
-            summed = nn(coulomb[0], polarized(0, e, part)) + nn(coulomb[2], polarized(2, e, part)) + middle
+            if part_of == last:
+                summed = total[e]
+            else:
+                summed = nn(coulomb[1], polarized(1, e, part_of)) + nn(coulomb[near], polarized(near, e, part_of))
+            summed = nn(coulomb[2 - near], polarized(2 - near, e, part_of)) + summed
             for c in range(2):
                 out[c, e, :, cols] = summed[:, c * LANES:(c + 1) * LANES].astype(BF16)
 

time: 66.1 us -> 65.9 us (level)
  no operation moved by 1% of the time
where the time goes in v5:
time: 65.9 us; the launch traced here: 65.8 us
  Pallas kernels  64.8 us (98%)
  local copies, waits for them, and re-layouts  0.97 us (1%)
    pallas_call x1, Pallas kernels, fused(): pl.pallas_call(functools.partial(fused_kernel, n, cells), out_shape=pltpu...  64.8 us

profile of v5, /device:TPU:1, one launch (start us, length us, event | category | flops | bytes accessed | tf_op | source)
XLA Modules:
  0.0 65.8 jit_solution(14842523033766854621)
XLA Ops:
  0.0 64.8 %shard_map.46 = bf16[2,4,256,256]{3,2,1,0:T(8,128)(2,1)S(1)} custom-call(bf16[2,4,256,256]{3,2,1,0:T(8,128)(2,1)} %bitcast.6, bf16[2,4,256,256]{3,2,1,0:T(8,128)(2,1)} %bitcast.7, bf16[2,4,256,256]{3,2,1,0:T(8,128)(2,1)} %bitcast.8, bf16[3,256,256]{2,1,0:T(8,128)(2,1)} %bitcast.9), custom_call_target="tpu_custom_call" | custom-call | tf_op jit(solution)/shard_map/pallas_call | solution.py:558
  64.8 1.0 %copy.6 = bf16[1,2,4,256,256]{4,3,2,1,0:T(8,128)(2,1)} copy(bf16[1,2,4,256,256]{4,3,2,1,0:T(8,128)(2,1)S(1)} %bitcast.5) | data formatting | bytes 2097152
